TPU v7x, 128 devices: a whole 4x4x4 slice. The times are simulated.
128 devices in a mesh: row: 4 (over y_lo, core), col: 32 (over x, z, y_hi).
Axes of the slice: x: 4, y: 4 (y_hi: 2, y_lo: 2; y = y_hi * 2 + y_lo), z: 4, core: 2. Of those that a mesh axis runs over, the one named last changes fastest.
Arguments:
- features: bfloat16 [65536, 256], P(('row', 'col')), may hold values from -6 to 6
- tile_values: bfloat16 [256, 64, 256, 256], P('col', 'row'), may hold values from 0 to 1, as said below
- tile_cols: int32 [256, 64], P('col', 'row'), may hold values from 0 to 63
- tile_counts: int32 [256, 4], P('col', 'row'), may hold values from 1 to 16, as said below
- weight: bfloat16 [256, 256], replicated, may hold values from -0.375 to 0.375
- bias: float32 [256], replicated, may hold values from -3 to 3
- cotangent: bfloat16 [65536, 256], P(('col', 'row')), may hold values from -6 to 6
Outputs:
- layer_out: bfloat16 [65536, 256], P(('col', 'row'))
- feature_grad: bfloat16 [65536, 256], P(('row', 'col'))
- weight_grad: float32 [256, 256], replicated
- bias_grad: float32 [256], replicated
Inputs may be any that keep to these rules, and one draw needn't show every extreme that they name: `tile_values`: nonnegative edge weights. `tile_counts`: every draw has some entry equal to 16; the loads differ between the devices' blocks.
All inputs are finite; a program needn't handle non-finite values.
Results may differ from a plain program's by a relative error of at most 0.025.
Values may be sent and summed in bfloat16 or wider, within the bound.
A program may use at most 128 MiB of HBM per device.

v0:
```python
import math
import jax
import jax.numpy as jnp
from jax import lax
from jax.sharding import PartitionSpec as P


def dense_part(hidden, weight, bias, cotangent):
    preact = jnp.dot(hidden, weight, preferred_element_type=jnp.float32) + bias
    output = jax.nn.silu(preact).astype(jnp.bfloat16)
    sigmoid_value = jax.nn.sigmoid(preact)
    slope = sigmoid_value * (1.0 + preact * (1.0 - sigmoid_value))
    preact_grad = (cotangent.astype(jnp.float32) * slope).astype(jnp.bfloat16)
    weight_grad = lax.dot_general(
        hidden, preact_grad, (((0,), (0,)), ((), ())), preferred_element_type=jnp.float32
    )
    bias_grad = jnp.sum(preact_grad.astype(jnp.float32), axis=0)
    hidden_grad = lax.dot_general(
        preact_grad, weight, (((1,), (1,)), ((), ())), preferred_element_type=jnp.float32
    ).astype(jnp.bfloat16)
    return (output, weight_grad, bias_grad, hidden_grad)


def per_device(features, tile_values, tile_cols, tile_counts, weight, bias, cotangent):
    node_dev, width = features.shape
    row_tiles, slot_count, tile_size, _ = tile_values.shape
    column_block = lax.all_gather(features, "col", axis=0, tiled=True)
    column_tiles = column_block.shape[0] // tile_size
    x_tiles = column_block.reshape(column_tiles, tile_size, width)
    live_counts = tile_counts[:, 0]
    slot_top = jnp.max(live_counts)

    def slot_data(slot):
        values = lax.dynamic_index_in_dim(tile_values, slot, 1, keepdims=False)
        columns = lax.dynamic_index_in_dim(tile_cols, slot, 1, keepdims=False)
        live = slot < live_counts
        return (values, columns, live)

    def forward_slot(slot, running):
        values, columns, live = slot_data(slot)
        picked = jnp.take(x_tiles, columns, axis=0) * live[:, None, None].astype(jnp.bfloat16)
        return running + jnp.einsum(
            "tij,tjf->tif", values, picked, preferred_element_type=jnp.float32
        )

    partial_value = lax.fori_loop(
        0, slot_top, forward_slot, jnp.zeros((row_tiles, tile_size, width), jnp.float32)
    )
    partial_value = partial_value.reshape(row_tiles * tile_size, width)
    node_total = node_dev * lax.axis_size("row") * lax.axis_size("col")
    grad_scale = 1.0 / math.sqrt(node_total)
    own_rows = lax.psum_scatter(
        partial_value.astype(jnp.bfloat16), "row", scatter_dimension=0, tiled=True
    )
    layer_out, weight_grad, bias_grad, hidden_grad = dense_part(own_rows, weight, bias, cotangent)
    weight_grad, bias_grad = lax.psum((weight_grad, bias_grad), ("row", "col"))
    grad_block = lax.all_gather(hidden_grad, "row", axis=0, tiled=True)
    grad_tiles = grad_block.reshape(row_tiles, tile_size, width)

    def backward_slot(slot, running):
        values, columns, live = slot_data(slot)
        contrib = jnp.einsum("tij,tif->tjf", values, grad_tiles, preferred_element_type=jnp.float32)
        contrib = contrib * live[:, None, None].astype(jnp.float32)
        return running.at[columns].add(contrib)

    summed = lax.fori_loop(
        0, slot_top, backward_slot, jnp.zeros((column_tiles, tile_size, width), jnp.float32)
    )
    summed = summed.reshape(column_tiles * tile_size, width)
    feature_grad = lax.psum_scatter(
        summed.astype(jnp.bfloat16), "col", scatter_dimension=0, tiled=True
    )
    return (layer_out, feature_grad, weight_grad * grad_scale, bias_grad * grad_scale)


def solution(mesh):
    placed = (
        P(("row", "col"), None),
        P("col", "row", None, None),
        P("col", "row"),
        P("col", "row"),
        P(),
        P(),
        P(("col", "row"), None),
    )
    return jax.shard_map(
        per_device,
        mesh=mesh,
        in_specs=placed,
        out_specs=(P(("col", "row"), None), P(("row", "col"), None), P(), P()),
        check_vma=False,
    )
```

profile of v0, /device:TPU:0, one launch (start us, length us, event | category | flops | bytes accessed | tf_op | source)
XLA Modules:
  0.0 641.1 jit_solution(3709168496130646856)
XLA Ops:
  8.0 0.8 copy.12
  8.7 1.3 reduce_max.9
  10.0 107.7 %all-gather.3.cloned.1.call-done = bf16[16384,256]{1,0:T(8,128)(2,1)} async-done(((bf16[512,256]{1,0:T(8,128)(2,1)}), bf16[16384,256]{1,0:T(8,128)(2,1)}) %all-gather.3.cloned.1.call-update) | async-done | bytes 8388624 | tf_op jit(solution)/shard_map/all_gather | solution.py:27
  118.0 60.5 %while.20 = (s32[]{:T(128)}, f32[8,256,256]{2,1,0:T(8,128)S(1)}, s32[]{:T(128)}, bf16[8,16,256,256]{3,2,1,0:T(8,128)(2,1)}, s32[8,16]{0,1:T(8,128)S(1)}, /*index...) while((s32[]{:T(128)}, f32[8,256,256]{2,1,0:T(8,128)S(1)}, s32[]{:T(128)}, ...), condition=%wide.region_2.3_spmd, body=%wide.region_1.2_spmd.sunk | while | flops 270009408 | bytes 8393067 | solution.py:46
  119.3 4.0 gather_fusion
  123.3 2.1 convolution_add_fusion.3
  126.8 4.0 gather_fusion
  130.8 2.1 convolution_add_fusion.3
  134.3 4.0 gather_fusion
  138.3 2.1 convolution_add_fusion.3
  141.7 4.0 gather_fusion
  145.8 2.1 convolution_add_fusion.3
  149.2 4.0 gather_fusion
  153.2 2.1 convolution_add_fusion.3
  156.7 4.0 gather_fusion
  160.7 2.1 convolution_add_fusion.3
  164.2 4.0 gather_fusion
  168.2 2.1 convolution_add_fusion.3
  171.7 4.0 gather_fusion
  175.7 2.1 convolution_add_fusion.3
  178.4 1.1 convert_element_type.43
  179.6 76.7 %reduce-scatter.3.cloned.1.call-done = bf16[512,256]{1,0:T(8,128)(2,1)} async-done(((bf16[2048,256]{1,0:T(8,128)(2,1)}), bf16[512,256]{1,0:T(8,128)(2,1)}) %reduce-scatter.3.cloned.1.call-update) | async-done | bytes 262160 | tf_op jit(solution)/shard_map/reduce_scatter | solution.py:52
  256.3 2.1 convert_reduce_fusion
  258.4 1.0 convolution_convert_fusion
  259.4 1.9 fusion.13
  261.4 20.0 %all-gather.5.cloned.1.call-done = bf16[2048,256]{1,0:T(8,128)(2,1)} async-done(((bf16[512,256]{1,0:T(8,128)(2,1)}), bf16[2048,256]{1,0:T(8,128)(2,1)}) %all-gather.5.cloned.1.call-update) | async-done | bytes 1048592 | tf_op jit(solution)/shard_map/all_gather | solution.py:57
  281.4 7.8 %broadcast_in_dim.21 = f32[64,256,256]{2,1,0:T(8,128)} broadcast(f32[]{:T(128)} %constant.49.clone.1), dimensions={} | broadcast | bytes 16777220 | tf_op jit(solution)/shard_map/broadcast_in_dim | solution.py:67
  289.2 55.6 %while.21 = (s32[]{:T(128)}, f32[64,256,256]{2,1,0:T(8,128)}, s32[]{:T(128)}, s32[8,16]{0,1:T(8,128)S(1)}, bf16[8,16,256,256]{3,2,1,0:T(8,128)(2,1)}, /*index=5*...) while((s32[]{:T(128)}, f32[64,256,256]{2,1,0:T(8,128)}, s32[]{:T(128)}, ...), condition=%wide.region_6.7_spmd, body=%wide.region_4.6_spmd.sunk | while | flops 269484064 | bytes 10486107 | solution.py:66
  289.9 1.8 convolution_multiply_fusion.2
  291.7 4.3 scatter_fusion
  296.7 1.8 convolution_multiply_fusion.2
  298.5 4.4 scatter_fusion
  303.6 1.8 convolution_multiply_fusion.2
  305.4 4.2 scatter_fusion
  310.3 1.8 convolution_multiply_fusion.2
  312.1 4.4 scatter_fusion
  317.2 1.8 convolution_multiply_fusion.2
  319.0 4.5 scatter_fusion
  324.2 1.8 convolution_multiply_fusion.2
  326.0 4.4 scatter_fusion
  331.1 1.8 convolution_multiply_fusion.2
  332.9 4.4 scatter_fusion
  338.0 1.8 convolution_multiply_fusion.2
  339.8 4.3 scatter_fusion
  344.8 9.0 %convert_element_type.49 = bf16[64,256,256]{2,1,0:T(8,128)(2,1)} convert(f32[64,256,256]{2,1,0:T(8,128)} %get-tuple-element.81) | non-fusion elementwise | flops 4194304 | bytes 25165824 | tf_op jit(solution)/shard_map/convert_element_type | solution.py:71
  353.8 162.3 %psum.15 = f32[256]{0:T(256)S(1)} all-reduce(f32[256]{0:T(256)S(1)} %get-tuple-element.126), channel_id=1, replica_groups=mesh['row'=4,'col'=32] {'row','col'}, use_global_device_ids=true, to_apply=%region_10.11 | all-reduce | flops 256 | bytes 2048 | tf_op jit(solution)/shard_map/psum | solution.py:56
  516.7 1.7 broadcast_multiply_fusion
  518.3 116.3 %reduce-scatter.5.cloned.1.call-done = bf16[512,256]{1,0:T(8,128)(2,1)} async-done(((bf16[16384,256]{1,0:T(8,128)(2,1)}), bf16[512,256]{1,0:T(8,128)(2,1)}) %reduce-scatter.5.cloned.1.call-update) | async-done | bytes 262160 | tf_op jit(solution)/shard_map/reduce_scatter | solution.py:70
  (61 shorter events, 7.3 us)
Async XLA Ops:
  7.2 249.1 %copy-start = (bf16[256,256]{1,0:T(8,128)(2,1)S(1)}, bf16[256,256]{1,0:T(8,128)(2,1)}, u32[]{:S(2)}) copy-start(bf16[256,256]{1,0:T(8,128)(2,1)} %param.15) | copy-start | bytes 393220
  7.2 110.6 %all-gather.3.cloned.1.call-start = ((), (), s32[]{:S(2)}) async-start(), calls=%async_computation.2 | async-start | bytes 8650752 | tf_op jit(solution)/shard_map/all_gather | solution.py:27
  7.9 248.3 %reduce-scatter.3.cloned.1.call-start = ((), (), s32[]{:S(2)}) async-start(), calls=%async_computation.3 | async-start | bytes 1310720 | tf_op jit(solution)/shard_map/reduce_scatter | solution.py:52
  118.0 138.3 %copy-start.2 = (f32[256]{0:T(256)S(1)}, f32[256]{0:T(256)}, u32[]{:S(2)}) copy-start(f32[256]{0:T(256)} %param.16) | copy-start | bytes 3076
  179.5 101.9 %all-gather.5.cloned.1.call-start = ((), (), s32[]{:S(2)}) async-start(), calls=%async_computation.4 | async-start | bytes 1310720 | tf_op jit(solution)/shard_map/all_gather | solution.py:57
  259.4 257.3 %all-reduce.2.cloned.1.call-start = ((), (), s32[]{:S(2)}) async-start(), calls=%async_computation.6 | async-start | bytes 524288 | tf_op jit(solution)/shard_map/psum | solution.py:56
  261.4 373.2 %reduce-scatter.5.cloned.1.call-start = ((), (), s32[]{:S(2)}) async-start(), calls=%async_computation.5 | async-start | bytes 8650752 | tf_op jit(solution)/shard_map/reduce_scatter | solution.py:70
  281.4 7.8 %copy-start.1 = (bf16[2048,256]{1,0:T(8,128)(2,1)S(1)}, bf16[2048,256]{1,0:T(8,128)(2,1)}, u32[]{:S(2)}) copy-start(bf16[2048,256]{1,0:T(8,128)(2,1)} %all-gather.5.cloned.1.call-done) | copy-start | bytes 3145732
  281.4 7.8 %copy-start.3 = (s32[8]{0:T(128)S(1)}, s32[8]{0:T(128)}, u32[]{:S(2)}) copy-start(s32[8]{0:T(128)} %get-tuple-element.303) | copy-start | bytes 100
Sparse Core Ops, SparseCore 0:
  11.0 106.7 all-gather.2
  179.7 76.5 reduce-scatter.2
  259.5 21.8 all-gather.4
  287.3 142.8 all-reduce.1
  433.1 201.3 reduce-scatter.4
where the time goes:
time: 644 us; the launch traced here: 641 us
  waiting for transfers between devices  321 us (50%)
  blocking collectives  162 us (25%)
  other arithmetic  54.1 us (8%)
  local copies, waits for them, and re-layouts  40.7 us (6%)
  matrix products  36.5 us (6%)
  between operations  13.8 us (2%)
  loops' own time  12.1 us (2%)
    psum x1, blocking collectives, per_device(): weight_grad, bias_grad = lax.psum((weight_grad, bias_grad), ('row', 'col'))  162 us
    reduce_scatter x1, waiting for transfers between devices, per_device(): lax.psum_scatter(summed.astype(jnp.bfloat16), 'col', scatter_dimension=0,...  116 us
    all_gather x1, waiting for transfers between devices, per_device(): column_block = lax.all_gather(features, 'col', axis=0, tiled=True)  108 us
    reduce_scatter x1, waiting for transfers between devices, per_device(): lax.psum_scatter(partial_value.astype(jnp.bfloat16), 'row', scatter_dimen...  76.7 us
    scatter-add x8, other arithmetic, backward_slot(): return running.at[columns].add(contrib)  34.9 us
    gather x8, local copies, waits for them, and re-layouts, forward_slot(): jnp.take(x_tiles, columns, axis=0)  32 us
    all_gather x1, waiting for transfers between devices, per_device(): grad_block = lax.all_gather(hidden_grad, 'row', axis=0, tiled=True)  20 us
    dot_general x8, matrix products, forward_slot(): jnp.einsum('tij,tjf->tif', values, picked, preferred_element_type=jnp.flo...  17 us
  transfers between devices with their start and end apart: 5, of which 4 were waited for; matrix products, arithmetic and copies ran while one was open for 11% of the time, Pallas kernels for 0%

commit v1 on v0

--- a/solution.py
+++ b/solution.py
@@ -1,8 +1,18 @@
+import functools
 import math
 import jax
 import jax.numpy as jnp
 from jax import lax
 from jax.sharding import PartitionSpec as P
+
+
+def run_layers_all_now(state, along_axis, group_axis):
+    for i in (along_axis, group_axis):
+        state = lax.psum(state, i)
+    return state
+
+
+_apply_values = functools.partial(run_layers_all_now, along_axis="col", group_axis="row")
 
 
 def dense_part(hidden, weight, bias, cotangent):
@@ -53,7 +63,7 @@
         partial_value.astype(jnp.bfloat16), "row", scatter_dimension=0, tiled=True
     )
     layer_out, weight_grad, bias_grad, hidden_grad = dense_part(own_rows, weight, bias, cotangent)
-    weight_grad, bias_grad = lax.psum((weight_grad, bias_grad), ("row", "col"))
+    weight_grad, bias_grad = _apply_values((weight_grad, bias_grad))
     grad_block = lax.all_gather(hidden_grad, "row", axis=0, tiled=True)
     grad_tiles = grad_block.reshape(row_tiles, tile_size, width)
 

time: 644 us -> 972 us (1.51)
  waiting for transfers between devices: 321 us -> 666 us
  blocking collectives: 162 us -> 147 us
    psum x1 -> x2, waiting for transfers between devices: 0.01 us -> 348 us  [run_layers_all_now(): state = lax.psum(state, i)]
    psum x1 -> x2, blocking collectives: 162 us -> 147 us  [run_layers_all_now(): state = lax.psum(state, i)]
  transfers between devices with their start and end apart: 5 -> 6, of which waited for: 4 -> 5; matrix products, arithmetic and copies ran while one was open for 11% -> 7% of each run, Pallas kernels for 0% -> 0%
where the time goes in v1:
time: 972 us; the launch traced here: 969 us
  waiting for transfers between devices  666 us (69%)
  blocking collectives  147 us (15%)
  other arithmetic  54 us (6%)
  local copies, waits for them, and re-layouts  40.7 us (4%)
  matrix products  36.5 us (4%)
  between operations  14.2 us (1%)
  loops' own time  10.8 us (1%)
    psum x2, waiting for transfers between devices, run_layers_all_now(): state = lax.psum(state, i)  348 us
    psum x2, blocking collectives, run_layers_all_now(): state = lax.psum(state, i)  147 us
    reduce_scatter x1, waiting for transfers between devices, per_device(): lax.psum_scatter(summed.astype(jnp.bfloat16), 'col', scatter_dimension=0,...  110 us
    all_gather x1, waiting for transfers between devices, per_device(): column_block = lax.all_gather(features, 'col', axis=0, tiled=True)  108 us
    reduce_scatter x1, waiting for transfers between devices, per_device(): lax.psum_scatter(partial_value.astype(jnp.bfloat16), 'row', scatter_dimen...  76.1 us
    scatter-add x8, other arithmetic, backward_slot(): return running.at[columns].add(contrib)  34.8 us
    gather x8, local copies, waits for them, and re-layouts, forward_slot(): jnp.take(x_tiles, columns, axis=0)  32 us
    all_gather x1, waiting for transfers between devices, per_device(): grad_block = lax.all_gather(hidden_grad, 'row', axis=0, tiled=True)  23.2 us
  transfers between devices with their start and end apart: 6, of which 5 were waited for; matrix products, arithmetic and copies ran while one was open for 7% of the time, Pallas kernels for 0%

profile of v1, /device:TPU:0, one launch (start us, length us, event | category | flops | bytes accessed | tf_op | source)
XLA Modules:
  0.0 969.5 jit_solution(18244868971362568857)
XLA Ops:
  8.7 1.3 reduce_max.9
  10.0 107.8 %all-gather.3.cloned.1.call-done = bf16[16384,256]{1,0:T(8,128)(2,1)} async-done(((bf16[512,256]{1,0:T(8,128)(2,1)}), bf16[16384,256]{1,0:T(8,128)(2,1)}) %all-gather.3.cloned.1.call-update) | async-done | bytes 8388624 | tf_op jit(solution)/shard_map/all_gather | solution.py:37
  118.0 59.8 %while.20 = (s32[]{:T(128)}, f32[8,256,256]{2,1,0:T(8,128)S(1)}, s32[]{:T(128)}, bf16[8,16,256,256]{3,2,1,0:T(8,128)(2,1)}, s32[8,16]{0,1:T(8,128)S(1)}, /*index...) while((s32[]{:T(128)}, f32[8,256,256]{2,1,0:T(8,128)S(1)}, s32[]{:T(128)}, ...), condition=%wide.region_2.3_spmd, body=%wide.region_1.2_spmd.sunk | while | flops 270009408 | bytes 8393067 | solution.py:56
  119.2 4.0 gather_fusion
  123.2 2.1 convolution_add_fusion.3
  126.6 4.0 gather_fusion
  130.6 2.1 convolution_add_fusion.3
  134.0 4.0 gather_fusion
  138.0 2.1 convolution_add_fusion.3
  141.4 4.0 gather_fusion
  145.4 2.1 convolution_add_fusion.3
  148.8 4.0 gather_fusion
  152.9 2.1 convolution_add_fusion.3
  156.3 4.0 gather_fusion
  160.3 2.1 convolution_add_fusion.3
  163.7 4.0 gather_fusion
  167.7 2.1 convolution_add_fusion.3
  171.1 4.0 gather_fusion
  175.1 2.1 convolution_add_fusion.3
  177.8 1.1 convert_element_type.43
  178.9 76.1 %reduce-scatter.3.cloned.1.call-done = bf16[512,256]{1,0:T(8,128)(2,1)} async-done(((bf16[2048,256]{1,0:T(8,128)(2,1)}), bf16[512,256]{1,0:T(8,128)(2,1)}) %reduce-scatter.3.cloned.1.call-update) | async-done | bytes 262160 | tf_op jit(solution)/shard_map/reduce_scatter | solution.py:62
  255.1 2.1 convert_reduce_fusion
  257.2 1.9 fusion.13
  260.3 348.1 %all-reduce.3.cloned.1.call-done = f32[256,256]{1,0:T(8,128)} async-done(((f32[256,256]{1,0:T(8,128)}), f32[256,256]{1,0:T(8,128)}) %all-reduce.3.cloned.1.call-update) | async-done | bytes 262160 | tf_op jit(solution)/shard_map/psum | solution.py:11
  608.4 23.2 %all-gather.5.cloned.1.call-done = bf16[2048,256]{1,0:T(8,128)(2,1)} async-done(((bf16[512,256]{1,0:T(8,128)(2,1)}), bf16[2048,256]{1,0:T(8,128)(2,1)}) %all-gather.5.cloned.1.call-update) | async-done | bytes 1048592 | tf_op jit(solution)/shard_map/all_gather | solution.py:67
  631.7 7.8 broadcast_in_dim.21
  639.4 54.8 %while.21 = (s32[]{:T(128)}, f32[64,256,256]{2,1,0:T(8,128)}, s32[]{:T(128)}, s32[8,16]{0,1:T(8,128)S(1)}, bf16[8,16,256,256]{3,2,1,0:T(8,128)(2,1)}, /*index=5*...) while((s32[]{:T(128)}, f32[64,256,256]{2,1,0:T(8,128)}, s32[]{:T(128)}, ...), condition=%wide.region_6.7_spmd, body=%wide.region_4.6_spmd.sunk | while | flops 269484064 | bytes 10486107 | solution.py:76
  640.1 1.8 convolution_multiply_fusion.2
  641.9 4.3 scatter_fusion
  646.8 1.8 convolution_multiply_fusion.2
  648.6 4.4 scatter_fusion
  653.6 1.8 convolution_multiply_fusion.2
  655.4 4.2 scatter_fusion
  660.3 1.8 convolution_multiply_fusion.2
  662.1 4.4 scatter_fusion
  667.1 1.8 convolution_multiply_fusion.2
  668.9 4.4 scatter_fusion
  673.9 1.8 convolution_multiply_fusion.2
  675.7 4.4 scatter_fusion
  680.7 1.8 convolution_multiply_fusion.2
  682.5 4.4 scatter_fusion
  687.5 1.8 convolution_multiply_fusion.2
  689.3 4.3 scatter_fusion
  694.2 9.0 convert_element_type.49
  703.2 137.8 %psum.30 = f32[256]{0:T(256)S(1)} all-reduce(f32[256]{0:T(256)S(1)} %get-tuple-element.126), channel_id=1, replica_groups=mesh['row'=4,'col'=32] {'col'}, use_global_device_ids=true, to_apply=%region_11.12 | all-reduce | flops 256 | bytes 2048 | tf_op jit(solution)/shard_map/psum | solution.py:11
  841.0 9.6 psum.31
  851.2 1.7 broadcast_multiply_fusion
  852.8 109.8 %reduce-scatter.5.cloned.1.call-done = bf16[512,256]{1,0:T(8,128)(2,1)} async-done(((bf16[16384,256]{1,0:T(8,128)(2,1)}), bf16[512,256]{1,0:T(8,128)(2,1)}) %reduce-scatter.5.cloned.1.call-update) | async-done | bytes 262160 | tf_op jit(solution)/shard_map/reduce_scatter | solution.py:80
  (65 shorter events, 9.1 us)
Async XLA Ops:
  7.2 247.9 %copy-start = (bf16[256,256]{1,0:T(8,128)(2,1)S(1)}, bf16[256,256]{1,0:T(8,128)(2,1)}, u32[]{:S(2)}) copy-start(bf16[256,256]{1,0:T(8,128)(2,1)} %param.15) | copy-start | bytes 393220
  7.2 110.6 %all-gather.3.cloned.1.call-start = ((), (), s32[]{:S(2)}) async-start(), calls=%async_computation.2 | async-start | bytes 8650752 | tf_op jit(solution)/shard_map/all_gather | solution.py:37
  7.9 247.2 %reduce-scatter.3.cloned.1.call-start = ((), (), s32[]{:S(2)}) async-start(), calls=%async_computation.3 | async-start | bytes 1310720 | tf_op jit(solution)/shard_map/reduce_scatter | solution.py:62
  118.0 137.1 %copy-start.2 = (f32[256]{0:T(256)S(1)}, f32[256]{0:T(256)}, u32[]{:S(2)}) copy-start(f32[256]{0:T(256)} %param.16) | copy-start | bytes 3076
  178.9 429.5 %all-reduce.3.cloned.1.call-start = ((), (), s32[]{:S(2)}) async-start(), calls=%async_computation.6 | async-start | bytes 524288 | tf_op jit(solution)/shard_map/psum | solution.py:11
  259.2 372.5 %all-gather.5.cloned.1.call-start = ((), (), s32[]{:S(2)}) async-start(), calls=%async_computation.4 | async-start | bytes 1310720 | tf_op jit(solution)/shard_map/all_gather | solution.py:67
  260.2 590.9 %all-reduce.5.cloned.1.call-start = ((), (), s32[]{:S(2)}) async-start(), calls=%async_computation.7 | async-start | bytes 524288 | tf_op jit(solution)/shard_map/psum | solution.py:11
  608.4 354.2 %reduce-scatter.5.cloned.1.call-start = ((), (), s32[]{:S(2)}) async-start(), calls=%async_computation.5 | async-start | bytes 8650752 | tf_op jit(solution)/shard_map/reduce_scatter | solution.py:80
  631.7 7.8 copy-start.1
  631.7 7.8 copy-start.3
Sparse Core Ops, SparseCore 0:
  11.0 106.7 all-gather.2
  179.0 76.0 reduce-scatter.2
  259.3 349.0 all-reduce.2
  610.5 21.1 all-gather.4
  634.0 36.9 all-reduce.4
  703.3 259.2 reduce-scatter.4
